TPU v7x, 32 devices: a whole 2x2x4 slice. The times are simulated.
32 devices in a mesh: section: 4 (over y, x), vocab: 8 (over z, core), dp: 1.
Axes of the slice: x: 2, y: 2, z: 4, core: 2. Of those that a mesh axis runs over, the one named last changes fastest.
Arguments:
- hidden: bfloat16 [1, 512, 3072], P('dp', ('section', 'vocab')), may hold values from -160 to 160
- head: bfloat16 [131072, 3072], P(('section', 'vocab')), may hold values from -3 to 3
- labels: int32 [1, 512], P('dp'), may hold values from 0 to 131071
- response_mask: int32 [1, 512], P('dp'), may hold values from 0 to 1, as said below
- seq_pair: int32 [1, 4], P('dp'), may hold values from 0 to 3, as said below
- ref_logp: float32 [4], replicated, may hold values from -12.6 to -12.4
Outputs:
- token_logprob: float32 [1, 512], P('dp', ('section', 'vocab'))
- pair_margin: float32 [2], replicated
- loss: float32 [], replicated
Inputs may be any that keep to these rules, and one draw needn't show every extreme that they name: `response_mask`: each sequence of 128 rows has more than half of its rows set. `seq_pair`: over all replicas every slot of 0 to 3 appears once; slot q belongs to pair q // 2 and is its chosen response when q is even.
All inputs are finite; a program needn't handle non-finite values.
Results may differ from a plain program's by a relative error of at most 0.0003.
Values may be sent and summed in bfloat16 or wider, within the bound.
A program may use at most 64 MiB of HBM per device.

v0:
```python
import jax
import jax.numpy as jnp
from jax import lax
from jax.sharding import PartitionSpec as P

SEQ_DP = 4
beta_scale = 5.0


def body(hidden, head, labels, response_mask, seq_pair, ref_logp):
    shard_rows = hidden.shape[1]
    vocab_rows = head.shape[0]
    chip_rows = lax.all_gather(hidden, "vocab", axis=1, tiled=True)
    gathered = lax.all_gather(chip_rows, "section", axis=1, tiled=True)
    logits = lax.dot_general(
        gathered[0], head, (((1,), (1,)), ((), ())), preferred_element_type=jnp.float32
    )
    position = lax.axis_index(("section", "vocab"))
    local_max = jnp.max(logits, axis=1)
    local_sum = jnp.sum(jnp.exp(logits - local_max[:, None]), axis=1)
    target = labels[0] - position * vocab_rows
    column = lax.broadcasted_iota(jnp.int32, logits.shape, 1)
    label_part = jnp.sum(jnp.where(column == target[:, None], logits, 0.0), axis=1)
    whole_max = lax.pmax(local_max, ("section", "vocab"))
    total, label_logit = lax.psum(
        (local_sum * jnp.exp(local_max - whole_max), label_part), ("section", "vocab")
    )
    logprob = label_logit - whole_max - jnp.log(total)
    own_rows = lax.dynamic_slice_in_dim(logprob, position * shard_rows, shard_rows)
    token_logprob = own_rows[None, :]
    all_rows = logprob.shape[0]
    seq_len = all_rows // SEQ_DP
    slot_count = ref_logp.shape[0]
    weights = response_mask[0].astype(jnp.float32)
    counts = jnp.sum(weights.reshape(SEQ_DP, seq_len), axis=1)
    slot_ids = lax.broadcasted_iota(jnp.int32, (SEQ_DP, slot_count), 1)
    in_pair = (seq_pair[0][:, None] == slot_ids).astype(jnp.float32)
    seq_sums = jnp.sum((logprob * weights).reshape(SEQ_DP, seq_len), axis=1)
    seq_means = seq_sums / counts
    policy = lax.psum(jnp.sum(in_pair * seq_means[:, None], axis=0), "dp")
    pair_margin = beta_scale * (policy[0::2] - ref_logp[0::2] - (policy[1::2] - ref_logp[1::2]))
    loss = jnp.mean(jnp.logaddexp(0.0, -pair_margin))
    return (token_logprob, pair_margin, loss)


def solution(mesh):
    placed = (
        P("dp", ("section", "vocab"), None),
        P(("section", "vocab"), None),
        P("dp", None),
        P("dp", None),
        P("dp", None),
        P(),
    )
    return jax.shard_map(
        body,
        mesh=mesh,
        in_specs=placed,
        out_specs=(P("dp", ("section", "vocab")), P(), P()),
        check_vma=False,
    )
```

profile of v0, /device:TPU:0, one launch (start us, length us, event | category | flops | bytes accessed | tf_op | source)
XLA Modules:
  0.0 187.5 jit_solution(17460948723642342068)
XLA Ops:
  7.2 0.0 all-gather.2.cloned.1.call-start
  7.2 18.5 %all_gather.6 = bf16[1,128,3072]{2,1,0:T(8,128)(2,1)} all-gather(bf16[1,16,3072]{2,1,0:T(8,128)(2,1)} %param.6), channel_id=1, replica_groups=mesh['section'=4,'vocab'=8,'dp'=1] {'vocab'}, dimensions={1}, use_global_device_ids=true | all-gather | bytes 884736 | tf_op jit(solution)/shard_map/all_gather | solution.py:13
  25.7 0.0 all-gather.2.cloned.1.call-update
  25.8 0.7 slice.13
  26.5 0.7 slice.15
  27.2 0.7 convert_element_type.15
  27.9 0.1 reduce_sum.57
  28.0 0.7 broadcast_subtract_fusion
  28.7 41.9 %all-gather.2.cloned.1.call-done = bf16[1,512,3072]{2,1,0:T(8,128)(2,1)} async-done(((bf16[1,128,3072]{2,1,0:T(8,128)(2,1)}), bf16[1,512,3072]{2,1,0:T(8,128)(2,1)}) %all-gather.2.cloned.1.call-update) | async-done | bytes 3145744 | tf_op jit(solution)/shard_map/all_gather | solution.py:14
  70.6 21.0 %fusion.3 = (f32[512]{0:T(512)S(1)}, f32[512,4096]{1,0:T(8,128)}) fusion(bf16[4096,3072]{1,0:T(8,128)(2,1)} %param.7, bf16[1,512,3072]{2,1,0:T(8,128)(2,1)} %all-gather.2.cloned.1.call-done), kind=kOutput, calls=%fused_computation.15 | convolution fusion | flops 12886999040 | bytes 36702208 | tf_op jit(solution)/shard_map/dot_general | solution.py:15
  91.6 0.0 copy-start
  91.6 39.2 %pmax.7 = f32[512]{0:T(512)S(1)} all-reduce(f32[512]{0:T(512)S(1)} %get-tuple-element.11), channel_id=1, replica_groups=mesh['section'=4,'vocab'=8,'dp'=1] {'section','vocab'}, use_global_device_ids=true, to_apply=%region_3.4 | all-reduce | flops 512 | bytes 4096 | tf_op jit(solution)/shard_map/pmax | solution.py:24
  130.9 4.9 %select_reduce_fusion = (f32[512]{0:T(512)S(1)}, f32[512]{0:T(512)S(1)}) fusion(f32[512,4096]{1,0:T(8,128)} %get-tuple-element.12, s32[512]{0:T(512)S(1)} %bitcast.16, f32[512]{0:T(512)S(1)} %get-tuple-element.11), kind=kLoop, calls=%fused_computation.1 | loop fusion | flops 10484736 | bytes 8396800 | tf_op jit(solution)/shard_map/reduce_sum | solution.py:23
  135.8 40.9 %all-reduce = (f32[512]{0:T(512)S(1)}, f32[512]{0:T(512)S(1)}) all-reduce(f32[512]{0:T(512)S(1)} %exponential_multiply_fusion, f32[512]{0:T(512)S(1)} %get-tuple-element.3), channel_id=1, replica_groups=mesh['section'=4,'vocab'=8,'dp'=1] {'section','vocab'}, use_global_device_ids=true, to_apply=%region_5.6 | all-reduce | flops 1024 | bytes 8192 | tf_op jit(solution)/shard_map/psum | solution.py:25
  176.8 0.1 bitcast_reduce_fusion
  176.9 0.0 copy-done
  176.9 0.1 select_reduce_fusion.1
  177.0 0.1 slice.12
  177.1 0.1 slice.14
  177.2 1.1 fusion.2
  178.9 0.6 dynamic-slice_bitcast_fusion
  (2 shorter events, 0.0 us)
Async XLA Ops:
  7.2 63.5 %all-gather.2.cloned.1.call-start = ((), (), s32[]{:S(2)}) async-start(), calls=%async_computation | async-start | bytes 3932160 | tf_op jit(solution)/shard_map/all_gather | solution.py:14
  91.6 85.3 %copy-start = (s32[1,4]{1,0:T(1,128)S(1)}, s32[1,4]{1,0:T(1,128)}, u32[]{:S(2)}) copy-start(s32[1,4]{1,0:T(1,128)} %param.10) | copy-start | bytes 52
Sparse Core Ops, SparseCore 0:
  25.9 44.7 all-gather.1
where the time goes:
time: 188 us
  blocking collectives  98.7 us (52%)
  waiting for transfers between devices  41.9 us (22%)
  matrix products  21 us (11%)
  between operations  15.8 us (8%)
  other arithmetic  7.75 us (4%)
  local copies, waits for them, and re-layouts  2.27 us (1%)
    all_gather x1, waiting for transfers between devices, body(): gathered = lax.all_gather(chip_rows, 'section', axis=1, tiled=True)  41.9 us
    psum x1, blocking collectives, body(): lax.psum((local_sum * jnp.exp(local_max - whole_max), label_part), ('sect...  40.9 us
    pmax x1, blocking collectives, body(): whole_max = lax.pmax(local_max, ('section', 'vocab'))  39.2 us
    dot_general x1, matrix products, body(): lax.dot_general(gathered[0], head, (((1,), (1,)), ((), ())), preferred_el...  21 us
    all_gather x1, blocking collectives, body(): chip_rows = lax.all_gather(hidden, 'vocab', axis=1, tiled=True)  18.5 us
    reduce_sum x1, other arithmetic, body(): jnp.sum(jnp.where(column == target[:, None], logits, 0.0), axis=1)  4.93 us
  transfers between devices with their start and end apart: 1, of which 1 were waited for; matrix products, arithmetic and copies ran while one was open for 2% of the time, Pallas kernels for 0%

commit v1 on v0

--- a/solution.py
+++ b/solution.py
@@ -23,7 +23,7 @@
     label_part = jnp.sum(jnp.where(column == target[:, None], logits, 0.0), axis=1)
     whole_max = lax.pmax(local_max, ("section", "vocab"))
     total, label_logit = lax.psum(
-        (local_sum * jnp.exp(local_max - whole_max), label_part), ("section", "vocab")
+        lax.psum((local_sum * jnp.exp(local_max - whole_max), label_part), "vocab"), "section"
     )
     logprob = label_logit - whole_max - jnp.log(total)
     own_rows = lax.dynamic_slice_in_dim(logprob, position * shard_rows, shard_rows)

time: 188 us -> 171 us (0.910)
  blocking collectives: 98.7 us -> 82 us
    psum x1 -> x2, blocking collectives: 40.9 us -> 24.3 us  [the longest x1 14.5 us: body(): lax.psum((local_sum * jnp.exp(local_max - whole_max), label_part), 'vocab')]
where the time goes in v1:
time: 171 us
  blocking collectives  82 us (48%)
  waiting for transfers between devices  41.9 us (25%)
  matrix products  21 us (12%)
  between operations  15.8 us (9%)
  other arithmetic  7.76 us (5%)
  local copies, waits for them, and re-layouts  2.27 us (1%)
    all_gather x1, waiting for transfers between devices, body(): gathered = lax.all_gather(chip_rows, 'section', axis=1, tiled=True)  41.9 us
    pmax x1, blocking collectives, body(): whole_max = lax.pmax(local_max, ('section', 'vocab'))  39.2 us
    dot_general x1, matrix products, body(): lax.dot_general(gathered[0], head, (((1,), (1,)), ((), ())), preferred_el...  21 us
    all_gather x1, blocking collectives, body(): chip_rows = lax.all_gather(hidden, 'vocab', axis=1, tiled=True)  18.5 us
    psum x1, blocking collectives, body(): lax.psum((local_sum * jnp.exp(local_max - whole_max), label_part), 'vocab')  14.5 us
    psum x1, blocking collectives, body(): lax.psum(lax.psum((local_sum * jnp.exp(local_max - whole_max), label_part...  9.78 us
    reduce_sum x1, other arithmetic, body(): jnp.sum(jnp.where(column == target[:, None], logits, 0.0), axis=1)  4.93 us
  transfers between devices with their start and end apart: 1, of which 1 were waited for; matrix products, arithmetic and copies ran while one was open for 2% of the time, Pallas kernels for 0%

profile of v1, /device:TPU:0, one launch (start us, length us, event | category | flops | bytes accessed | tf_op | source)
XLA Modules:
  0.0 170.8 jit_solution(14229816717757317643)
XLA Ops:
  7.2 0.0 all-gather.2.cloned.1.call-start
  7.2 18.5 %all_gather.6 = bf16[1,128,3072]{2,1,0:T(8,128)(2,1)} all-gather(bf16[1,16,3072]{2,1,0:T(8,128)(2,1)} %param.6), channel_id=1, replica_groups=mesh['section'=4,'vocab'=8,'dp'=1] {'vocab'}, dimensions={1}, use_global_device_ids=true | all-gather | bytes 884736 | tf_op jit(solution)/shard_map/all_gather | solution.py:13
  25.7 0.0 all-gather.2.cloned.1.call-update
  25.8 0.7 slice.13
  26.5 0.7 slice.15
  27.2 0.7 convert_element_type.15
  27.9 0.1 reduce_sum.57
  28.0 0.7 broadcast_subtract_fusion
  28.7 41.9 %all-gather.2.cloned.1.call-done = bf16[1,512,3072]{2,1,0:T(8,128)(2,1)} async-done(((bf16[1,128,3072]{2,1,0:T(8,128)(2,1)}), bf16[1,512,3072]{2,1,0:T(8,128)(2,1)}) %all-gather.2.cloned.1.call-update) | async-done | bytes 3145744 | tf_op jit(solution)/shard_map/all_gather | solution.py:14
  70.6 21.0 %fusion.3 = (f32[512]{0:T(512)S(1)}, f32[512,4096]{1,0:T(8,128)}) fusion(bf16[4096,3072]{1,0:T(8,128)(2,1)} %param.7, bf16[1,512,3072]{2,1,0:T(8,128)(2,1)} %all-gather.2.cloned.1.call-done), kind=kOutput, calls=%fused_computation.15 | convolution fusion | flops 12886999040 | bytes 36702208 | tf_op jit(solution)/shard_map/dot_general | solution.py:15
  91.6 0.0 copy-start
  91.6 39.2 %pmax.7 = f32[512]{0:T(512)S(1)} all-reduce(f32[512]{0:T(512)S(1)} %get-tuple-element.13), channel_id=1, replica_groups=mesh['section'=4,'vocab'=8,'dp'=1] {'section','vocab'}, use_global_device_ids=true, to_apply=%region_4.5 | all-reduce | flops 512 | bytes 4096 | tf_op jit(solution)/shard_map/pmax | solution.py:24
  130.9 4.9 %select_reduce_fusion = (f32[512]{0:T(512)S(1)}, f32[512]{0:T(512)S(1)}) fusion(f32[512,4096]{1,0:T(8,128)} %get-tuple-element.14, s32[512]{0:T(512)S(1)} %bitcast.16, f32[512]{0:T(512)S(1)} %get-tuple-element.13), kind=kLoop, calls=%fused_computation.1 | loop fusion | flops 10484736 | bytes 8396800 | tf_op jit(solution)/shard_map/reduce_sum | solution.py:23
  135.8 14.5 %all-reduce = (f32[512]{0:T(512)S(1)}, f32[512]{0:T(512)S(1)}) all-reduce(f32[512]{0:T(512)S(1)} %exponential_multiply_fusion, f32[512]{0:T(512)S(1)} %get-tuple-element.3), channel_id=1, replica_groups=mesh['section'=4,'vocab'=8,'dp'=1] {'vocab'}, use_global_device_ids=true, to_apply=%region_6.7 | all-reduce | flops 1024 | bytes 8192 | tf_op jit(solution)/shard_map/psum | solution.py:26
  150.3 9.8 %all-reduce.1 = (f32[512]{0:T(512)S(1)}, f32[512]{0:T(512)S(1)}) all-reduce(f32[512]{0:T(512)S(1)} %get-tuple-element.5, f32[512]{0:T(512)S(1)} %get-tuple-element.6), channel_id=1, replica_groups=mesh['section'=4,'vocab'=8,'dp'=1] {'section'}, use_global_device_ids=true, to_apply=%region_7.8 | all-reduce | flops 1024 | bytes 8192 | tf_op jit(solution)/shard_map/psum | solution.py:25
  160.1 0.1 bitcast_reduce_fusion
  160.2 0.0 copy-done
  160.2 0.1 select_reduce_fusion.1
  160.3 0.1 slice.12
  160.4 0.1 slice.14
  160.5 1.1 fusion.2
  162.3 0.6 dynamic-slice_bitcast_fusion
  (2 shorter events, 0.0 us)
Async XLA Ops:
  7.2 63.5 %all-gather.2.cloned.1.call-start = ((), (), s32[]{:S(2)}) async-start(), calls=%async_computation | async-start | bytes 3932160 | tf_op jit(solution)/shard_map/all_gather | solution.py:14
  91.6 68.6 %copy-start = (s32[1,4]{1,0:T(1,128)S(1)}, s32[1,4]{1,0:T(1,128)}, u32[]{:S(2)}) copy-start(s32[1,4]{1,0:T(1,128)} %param.10) | copy-start | bytes 52
Sparse Core Ops, SparseCore 0:
  25.9 44.7 all-gather.1
